TPU v7x, 256 devices: a whole 4x4x8 slice. The times are simulated.
256 devices in a mesh: qry: 16 (over y, z_hi), ref: 16 (over z_lo, x, core).
Axes of the slice: x: 4, y: 4, z: 8 (z_hi: 4, z_lo: 2; z = z_hi * 2 + z_lo), core: 2. Of those that a mesh axis runs over, the one named last changes fastest.
Arguments:
- series: float32 [1572864], P(('qry', 'ref')), may hold values from -20 to 20
Outputs:
- profile: float32 [1572864], P(('qry', 'ref'))
All inputs are finite; a program needn't handle non-finite values.
Results may differ from a plain program's by a relative error of at most 0.0013.
Values sent between devices are 32-bit elements; how exact they have to be, the bound alone decides.
A program may use at most 192 MiB of HBM per device.

v0:
```python
import math

import jax
import jax.numpy as jnp
from jax import lax
from jax.sharding import PartitionSpec as P

M = 1024
TILE = 512
PASSES = 2


def from_behind(block, axis, distance):
    devices = range(lax.axis_size(axis))
    route = [(i - distance, i) for i in devices if i - distance in devices]
    return lax.ppermute(block, axis, route)


def from_behind_2(value, axis, steps):
    count = lax.axis_size(axis)
    pairs = [(source, (source + steps) % count) for source in range(count)]
    return lax.ppermute(value, axis, pairs)


def hankel_rows(samples, count, width):
    length = count + width
    tiled = jnp.tile(samples, count + 1)[: count * (length + 1)]
    return tiled.reshape(count, length + 1)[:, :width]


def standardize(samples, count, width):
    block = min(count, 512)

    def one_block(index):
        piece = lax.dynamic_slice_in_dim(samples, index * block, block + width)
        shifted = piece - jnp.mean(piece)
        zero = jnp.zeros_like(shifted[:1])
        first = jnp.concatenate([zero, jnp.cumsum(shifted)])
        second = jnp.concatenate([zero, jnp.cumsum(shifted * shifted)])
        centre = (first[width : width + block] - first[:block]) / width
        power = (second[width : width + block] - second[:block]) / width
        spread = jnp.maximum(power - centre * centre, 0.0)
        factor = lax.rsqrt(spread + 1e-05) * (1.0 / math.sqrt(width))
        rows = hankel_rows(shifted, block, width)
        return ((rows - centre[:, None]) * factor[:, None]).astype(jnp.bfloat16)

    stacked = lax.map(one_block, jnp.arange(count // block, dtype=jnp.int32))
    return stacked.reshape(count, width)


def per_device(series):
    seg = series.shape[0]
    blocks = seg // TILE
    count_ref = lax.axis_size("ref")
    count_qry = lax.axis_size("qry")
    total = seg * count_ref * count_qry
    valid = total - M + 1
    q_index = lax.axis_index("qry")
    r_index = lax.axis_index("ref")
    tail = from_behind(series[:M], ("qry", "ref"), -1)
    samples = jnp.concatenate([series, tail])
    query = standardize(samples, seg, M)
    query_tiles = query.reshape(blocks, TILE, M)
    cols_local = jnp.arange(seg, dtype=jnp.int32)
    working = q_index < count_qry - 1
    fetched = []
    current = from_behind(samples, "qry", -1)
    fetched.append(current)
    offset = 1
    current = from_behind_2(current, "ref", -1)
    fetched.append(current)
    rowpart = jnp.full((seg,), -1.0, jnp.float32)
    colparts = []
    for offset in range(PASSES):
        refs = standardize(fetched[offset], seg, M)
        ref_tiles = refs.reshape(blocks, TILE, M)
        corr = jnp.einsum(
            "tak,tbk->tab", query_tiles, ref_tiles, preferred_element_type=jnp.float32
        )
        target = (q_index + 1) * count_ref + (r_index + offset) % count_ref
        keep = ((target * seg + cols_local < valid) & working).reshape(blocks, TILE)
        corr = jnp.where(keep[:, None, :], corr, jnp.float32(-1.0))
        rowpart = jnp.maximum(rowpart, jnp.max(corr, axis=2).reshape(seg))
        colparts.append(jnp.max(corr, axis=1).reshape(seg))
    colacc = colparts[0]
    offset = 1
    rolled = from_behind_2(colparts[offset], "ref", offset)
    colacc = jnp.maximum(colacc, rolled)
    received = from_behind(colacc, "qry", 1)
    colprof = jnp.where(q_index >= 1, received, jnp.float32(-1.0))
    return jnp.maximum(rowpart, colprof)


def solution(mesh):
    placed = (P(("qry", "ref")),)
    return jax.shard_map(
        per_device, mesh=mesh, in_specs=placed, out_specs=P(("qry", "ref")), check_vma=False
    )
```

profile of v0, /device:TPU:24, one launch (start us, length us, event | category | flops | bytes accessed | tf_op | source)
XLA Modules:
  0.0 652.6 jit_solution(12733739449241904078)
XLA Ops:
  0.7 9.6 %collective-permute-start = (f32[1024]{0:T(1024)S(1)}, f32[1024]{0:T(1024)S(1)}, u32[]{:S(2)}, u32[]{:S(2)}) collective-permute-start(f32[1024]{0:T(1024)S(1)} %slice.99), channel_id=1, source_target_pairs={{1,0},{2,1},{3,2},{4,3},{5,4},{6,5},{7,6},{8,7},{9,8},{10,9},{11,1... | collective-permute-start | bytes 12296 | tf_op jit(solution)/shard_map/ppermute | solution.py:16
  15.6 6.2 broadcast.129.clone
  21.8 196.5 %while.30 = (s32[]{:T(128)}, bf16[12,512,1024]{2,1,0:T(8,128)(2,1)}, s32[12]{0:T(128)S(1)}, f32[7168]{0:T(1024)}, s32[]{:T(128)}, /*index=5*/s32[1]{0:T(128)}, s...) while((s32[]{:T(128)}, bf16[12,512,1024]{2,1,0:T(8,128)(2,1)}, s32[12]{0:T(128)S(1)}, ...), condition=%wide.region_6.7_spmd, body=%wide.region_0.6_spmd.sunk | while | flops 1976612 | bytes 25302400 | solution.py:47
  31.3 4.1 reshape.146
  47.7 4.1 reshape.146
  64.1 4.1 reshape.146
  80.4 4.1 reshape.146
  96.8 4.1 reshape.146
  113.2 4.1 reshape.146
  129.6 4.1 reshape.146
  145.9 4.1 reshape.146
  162.3 4.1 reshape.146
  178.7 4.1 reshape.146
  195.0 4.1 reshape.146
  218.3 5.6 collective-permute-start.2
  223.9 6.1 broadcast.129.clone.2
  230.0 198.8 %while.31 = (s32[]{:T(128)}, bf16[12,512,1024]{2,1,0:T(8,128)(2,1)}, s32[12]{0:T(128)S(1)}, f32[7168]{0:T(1024)}, s32[]{:T(128)}, /*index=5*/s32[1]{0:T(128)}, s...) while((s32[]{:T(128)}, bf16[12,512,1024]{2,1,0:T(8,128)(2,1)}, s32[12]{0:T(128)S(1)}, ...), condition=%wide.region_13.14_spmd, body=%wide.region_7.13_spmd.sunk | while | flops 1976612 | bytes 25302400 | solution.py:47
  239.6 4.1 reshape.147
  256.2 4.1 reshape.147
  272.8 4.1 reshape.147
  322.5 4.1 reshape.147
  339.1 4.1 reshape.147
  355.6 4.1 reshape.147
  372.2 4.1 reshape.147
  388.7 4.1 reshape.147
  405.3 4.1 reshape.147
  421.8 4.1 reshape.147
  428.8 6.2 broadcast.129.clone.1
  435.0 181.0 %while.32 = (s32[]{:T(128)}, bf16[12,512,1024]{2,1,0:T(8,128)(2,1)}, s32[12]{0:T(128)S(1)}, f32[7168]{0:T(1024)S(1)}, s32[]{:T(128)}, /*index=5*/s32[1]{0:T(128)...) while((s32[]{:T(128)}, bf16[12,512,1024]{2,1,0:T(8,128)(2,1)}, s32[12]{0:T(128)S(1)}, ...), condition=%wide.region_21.22_spmd, body=%wide.region_15.21_spmd.sunk | while | flops 1976612 | bytes 25302400 | solution.py:47
  615.9 13.5 %select_reduce_fusion = (f32[12,512]{1,0:T(8,128)S(1)}, f32[12,512]{1,0:T(8,128)S(1)}) fusion(pred[12,512]{1,0:T(8,128)(4,1)S(1)} %get-tuple-element.121, bf16[12,512,1024]{2,1,0:T(8,128)(2,1)} %get-tuple-element.71, bf16[12,512,1024]{2,1,0:T(8,128)(2,1)} %get-tuple-element.73), kind=kOutput, calls=%fused_computation.69 | convolution fusion | flops 6451875840 | bytes 25221120 | tf_op jit(solution)/shard_map/tak,tbk->tab/dot_general | solution.py:77
  629.7 13.5 %select_reduce_fusion.2 = (f32[12,512]{1,0:T(8,128)S(1)}, f32[12,512]{1,0:T(8,128)S(1)}) fusion(pred[12,512]{1,0:T(8,128)(4,1)S(1)} %get-tuple-element.120, bf16[12,512,1024]{2,1,0:T(8,128)(2,1)} %get-tuple-element.71, bf16[12,512,1024]{2,1,0:T(8,128)(2,1)} %get-tuple-element.72), kind=kOutput, calls=%fused_computation.71 | convolution fusion | flops 6451875840 | bytes 25221120 | tf_op jit(solution)/shard_map/tak,tbk->tab/dot_general | solution.py:77
  645.2 6.8 %collective-permute-done.4 = f32[6144]{0:T(1024)S(1)} collective-permute-done((f32[6144]{0:T(1024)S(1)}, f32[6144]{0:T(1024)S(1)}, u32[]{:S(2)}, u32[]{:S(2)}) %collective-permute-start.4) | collective-permute-done | bytes 24608 | tf_op jit(solution)/shard_map/ppermute | solution.py:16
  (647 shorter events, 453.5 us)
Async XLA Ops:
  0.7 11.0 %collective-permute-start = (f32[1024]{0:T(1024)S(1)}, f32[1024]{0:T(1024)S(1)}, u32[]{:S(2)}, u32[]{:S(2)}) collective-permute-start(f32[1024]{0:T(1024)S(1)} %slice.99), channel_id=1, source_target_pairs={{1,0},{2,1},{3,2},{4,3},{5,4},{6,5},{7,6},{8,7},{9,8},{10,9},{11,1... | collective-permute-start | bytes 12296 | tf_op jit(solution)/shard_map/ppermute | solution.py:16
  12.3 206.1 %collective-permute-start.1 = (f32[7168]{0:T(1024)}, f32[7168]{0:T(1024)}, u32[]{:S(2)}, u32[]{:S(2)}) collective-permute-start(f32[7168]{0:T(1024)} %constant_dynamic-update-slice_fusion), channel_id=1, source_target_pairs={{16,0},{32,16},{48,32},{64,48},{80,64},{96,80},{112,96},{128,112},... | collective-permute-start | bytes 86024 | tf_op jit(solution)/shard_map/ppermute | solution.py:16
  218.3 210.4 %collective-permute-start.2 = (f32[7168]{0:T(1024)}, f32[7168]{0:T(1024)S(1)}, u32[]{:S(2)}, u32[]{:S(2)}) collective-permute-start(f32[7168]{0:T(1024)} %collective-permute-done.1), channel_id=1, source_target_pairs={{0,15},{1,0},{2,1},{3,2},{4,3},{5,4},{6,5},{7,6},{8,7},{9,8},{10,9... | collective-permute-start | bytes 86024 | tf_op jit(solution)/shard_map/ppermute | solution.py:22
  629.4 13.8 %collective-permute-start.3 = (f32[6144]{0:T(1024)S(1)}, f32[6144]{0:T(1024)S(1)}, u32[]{:S(2)}, u32[]{:S(2)}) collective-permute-start(f32[6144]{0:T(1024)S(1)} %reshape.136), channel_id=1, source_target_pairs={{0,1},{1,2},{2,3},{3,4},{4,5},{5,6},{6,7},{7,8},{8,9},{9,10},{10,1... | collective-permute-start | bytes 73736 | tf_op jit(solution)/shard_map/ppermute | solution.py:22
  643.3 8.7 %collective-permute-start.4 = (f32[6144]{0:T(1024)S(1)}, f32[6144]{0:T(1024)S(1)}, u32[]{:S(2)}, u32[]{:S(2)}) collective-permute-start(f32[6144]{0:T(1024)S(1)} %max.23), channel_id=1, source_target_pairs={{0,16},{16,32},{32,48},{48,64},{64,80},{80,96},{96,112},{112,128},... | collective-permute-start | bytes 73736 | tf_op jit(solution)/shard_map/ppermute | solution.py:16
where the time goes:
time: 658 us; the launch traced here: 653 us
  local copies, waits for them, and re-layouts  359 us (55%)
  other arithmetic  193 us (29%)
  loops' own time  45.8 us (7%)
  matrix products  27 us (4%)
  starting transfers between devices  20.7 us (3%)
  waiting for transfers between devices  6.78 us (1%)
    reshape x36, local copies, waits for them, and re-layouts, hankel_rows(): return tiled.reshape(count, length + 1)[:, :width]  147 us
    dynamic_update_slice x36, other arithmetic, standardize(): stacked = lax.map(one_block, jnp.arange(count // block, dtype=jnp.int32))  103 us
    another operation x72, local copies, waits for them, and re-layouts, hankel_rows(): tiled = jnp.tile(samples, count + 1)[:count * (length + 1)]  81.3 us
    slice x36, local copies, waits for them, and re-layouts, hankel_rows(): tiled = jnp.tile(samples, count + 1)[:count * (length + 1)]  75.4 us
    another operation x3, loops' own time, standardize(): stacked = lax.map(one_block, jnp.arange(count // block, dtype=jnp.int32))  45.8 us
    another operation x216, other arithmetic  45.3 us
    reduce_sum x36, other arithmetic, one_block(): shifted = piece - jnp.mean(piece)  41.4 us
    another operation x135, local copies, waits for them, and re-layouts  31.3 us
  transfers between devices with their start and end apart: 5, of which 1 were waited for; matrix products, arithmetic and copies ran while one was open for 60% of the time, Pallas kernels for 0%

commit v1 on v0

v1 whole, which is shorter than its diff:
```python
import functools

import jax
import jax.numpy as jnp
import numpy as np
from jax import lax
from jax.experimental import pallas as pl
from jax.experimental.pallas import tpu as pltpu
from jax.sharding import PartitionSpec as P

M = 1024
TILE = 512
L = 128
F32 = jnp.float32
BF16 = jnp.bfloat16
MESH = pl.DeviceIdType.MESH
BIG = 1e30


def split3(v):
    hi = v.astype(BF16)
    rest = v - hi.astype(F32)
    mid = rest.astype(BF16)
    low = (rest - mid.astype(F32)).astype(BF16)
    return hi, mid, low


def centre_tiles(src, dst, sums, tiles):
    sums[...] = jnp.broadcast_to(jnp.sum(src[...], axis=1, keepdims=True), src.shape)
    for t in range(tiles):
        c = sums[4 * t + 4 : 4 * t + 5] + sums[4 * t + 5 : 4 * t + 6]
        c = c + (sums[4 * t + 6 : 4 * t + 7] + sums[4 * t + 7 : 4 * t + 8])
        c = c * (1.0 / TILE)
        dst[16 * t : 16 * t + 12] = src[4 * t : 4 * t + 12] - c
        dst[16 * t + 12 : 16 * t + 16] = jnp.zeros((4, L), F32)


def window_stats(dst, ones, rb, r1, r2, total_row, scale_row, tiles):
    v = dst[...]
    w = ones[...]
    hi, mid, low = split3(v)
    dot = functools.partial(jnp.dot, preferred_element_type=F32)
    base = dot(hi, w)
    rb[...] = base
    r1[...] = base + (dot(mid, w) + dot(low, w))
    q_hi, q_mid, q_low = split3(v * v)
    r2[...] = dot(q_hi, w) + (dot(q_mid, w) + dot(q_low, w))
    dst[...] = hi.astype(F32)

    def window_sum(ref, t):
        b = 16 * t
        s = ref[b : b + 4, 0:L] + ref[b + 8 : b + 12, L : 2 * L]
        full = ref[b + 1 : b + 5, 2 * L : 3 * L]
        for r in range(2, 8):
            full = full + ref[b + r : b + r + 4, 2 * L : 3 * L]
        return s + full

    for t in range(tiles):
        total_row[4 * t : 4 * t + 4] = window_sum(rb, t)
        mean = window_sum(r1, t) * (1.0 / M)
        power = window_sum(r2, t) * (1.0 / M)
        spread = jnp.maximum(power - mean * mean, 0.0)
        scale_row[4 * t : 4 * t + 4] = lax.rsqrt(spread + 1e-05) * (1.0 / M**0.5)


def shear(rows, base, out, masks, first, store):
    wide = [
        jnp.broadcast_to(rows[pl.ds(base + m, 1), :], (16, L)).astype(BF16) for m in range(12)
    ]
    for g in range(8):
        mask = masks[16 * g : 16 * g + 16, :] > 0
        turned = [
            pltpu.roll(w, (first + 16 * g) % L, 1, stride=1, stride_axis=0) for w in wide
        ]
        for m in range(11):
            store(out, g, m, jnp.where(mask, turned[m], turned[m + 1]))


def kernel(
    x_ref, ones, anti, xmask, ymask, out_ref,
    xf, y0, y1, sums, xs, ys0, ys1, rb, r1, r2,
    xtot, xscale, ytot0, yscale0, ytot1, yscale1, lim0, lim1,
    lx, mcol, fcol, ha0, ha1, hb0, hb1, s0, s1, racc, col0, col1, got0, got1,
    send_sem, recv_sem,
):
    tiles = x_ref.shape[0] // 4
    rows = x_ref.shape[0]
    q = lax.axis_index("qry")
    r = lax.axis_index("ref")
    nq = lax.axis_size("qry")
    nr = lax.axis_size("ref")
    valid = nq * nr * rows * L - M + 1

    def wrap(a, n):
        return lax.rem(a + 2 * n, n)

    def at(flat):
        flat = lax.rem(flat + nq * nr, nq * nr)
        return flat // nr, lax.rem(flat, nr)

    me = q * nr + r
    nextq = wrap(q + 1, nq)
    nextr = wrap(r + 1, nr)
    prevq = wrap(q - 1, nq)
    prevr = wrap(r - 1, nr)
    after = at(me + 1)
    before = at(me - 1)
    tail0 = at(nextq * nr + r + 1)
    tail1 = at(nextq * nr + nextr + 1)
    sources = [after, (nextq, r), (nextq, nextr), tail0, tail1, (prevq, r), (prevq, prevr)]
    barrier = pltpu.get_barrier_semaphore()
    for source in sources:
        pl.semaphore_signal(barrier, inc=1, device_id=source, device_id_type=MESH)

    back = wrap(before[0] - 1, nq)
    head = x_ref.at[pl.ds(0, 8)]
    plan = [
        (head, xf.at[pl.ds(rows, 8)], before),
        (x_ref, y0.at[pl.ds(0, rows)], (prevq, r)),
        (x_ref, y1.at[pl.ds(0, rows)], (prevq, prevr)),
        (head, y0.at[pl.ds(rows, 8)], (back, before[1])),
        (head, y1.at[pl.ds(rows, 8)], (back, wrap(before[1] - 1, nr))),
        (col0, got0, (nextq, r)),
        (col1, got1, (nextq, nextr)),
    ]
    copies = [
        pltpu.make_async_remote_copy(
            src_ref=src, dst_ref=dst, send_sem=send_sem.at[n], recv_sem=recv_sem.at[n],
            device_id=device, device_id_type=MESH,
        )
        for n, (src, dst, device) in enumerate(plan)
    ]
    pl.semaphore_wait(barrier, len(sources))
    for c in copies[:5]:
        c.start()
    xf[0:rows, :] = x_ref[...]
    copies[0].wait()
    centre_tiles(xf, xs, sums, tiles)
    window_stats(xs, ones, rb, r1, r2, xtot, xscale, tiles)
    xs[...] = jnp.dot(xs[...].astype(BF16), anti[...], preferred_element_type=F32)

    def prepare(t, carry):
        def put(out, g, m, v):
            out[t, 16 * g : 16 * g + 16, L * m : L * m + L] = v

        shear(xs, 16 * t, lx, xmask, 0, put)
        for i in range(4):
            mean = xtot[pl.ds(4 * t + i, 1), :] * (1.0 / M)
            mcol[t, L * i : L * i + L, :] = jnp.transpose(jnp.broadcast_to(mean, (L, L)))
            scale = xscale[pl.ds(4 * t + i, 1), :]
            fcol[t, L * i : L * i + L, :] = jnp.transpose(jnp.broadcast_to(scale, (L, L)))
        return carry

    lax.fori_loop(0, tiles, prepare, 0)

    for c in copies[1:5]:
        c.wait()
    cell = lax.broadcasted_iota(jnp.int32, (rows, L), 0) * L
    cell = cell + lax.broadcasted_iota(jnp.int32, (rows, L), 1)
    for y, ys, ytot, yscale, lim, place in (
        (y0, ys0, ytot0, yscale0, lim0, r), (y1, ys1, ytot1, yscale1, lim1, nextr)
    ):
        centre_tiles(y, ys, sums, tiles)
        window_stats(ys, ones, rb, r1, r2, ytot, yscale, tiles)
        start = ((q + 1) * nr + place) * (rows * L)
        lim[...] = jnp.where(start + cell < valid, BIG, -BIG)

    def put(out, g, m, v):
        out[16 * g : 16 * g + 16, L * m : L * m + L] = v

    def build(t, h0, h1):
        shear(ys0, 16 * t, h0, ymask, 1, put)
        shear(ys1, 16 * t, h1, ymask, 1, put)

    def products(t, h, s):
        left = jnp.concatenate(
            [lx[t, :, L * i : L * i + M] for i in range(4)], axis=0
        )
        right = jnp.concatenate(
            [h[:, L * k : L * k + TILE] for k in range(8)], axis=0
        )
        s[...] = jnp.dot(left, right, preferred_element_type=F32)

    def maxima(t, s, ytot, yscale, lim, col, first):
        spread = lambda ref, j: jnp.broadcast_to(ref[pl.ds(4 * t + j, 1), :], (8, L))
        total = [spread(ytot, j) for j in range(4)]
        scale = [spread(yscale, j) for j in range(4)]
        bound = [spread(lim, j) for j in range(4)]
        best = [None] * 4
        for g in range(TILE // 8):
            part = pl.ds(8 * g, 8)
            mean = mcol[t, part, :]
            factor = fcol[t, part, :]
            row = None if first else racc[part, :]
            for j in range(4):
                v = s[part, L * j : L * j + L] - mean * total[j]
                a = jnp.minimum(v * scale[j], bound[j])
                row = a if row is None else jnp.maximum(row, a)
                b = v * factor
                best[j] = b if best[j] is None else jnp.maximum(best[j], b)
            racc[part, :] = row
        for j in range(4):
            top = jnp.max(best[j], axis=0, keepdims=True)
            top = jnp.maximum(top * yscale[pl.ds(4 * t + j, 1), :], -1.0)
            top = jnp.minimum(top, lim[pl.ds(4 * t + j, 1), :])
            col[pl.ds(4 * t + j, 1), :] = jnp.maximum(top, -1.0)

    def finish(t):
        for i in range(4):
            top = jnp.max(jnp.transpose(racc[L * i : L * i + L, :]), axis=0, keepdims=True)
            out_ref[pl.ds(4 * t + i, 1), :] = top * xscale[pl.ds(4 * t + i, 1), :]

    def one(t, h0, h1):
        products(t, h0, s0)
        products(t, h1, s1)
        maxima(t, s0, ytot0, yscale0, lim0, col0, True)
        maxima(t, s1, ytot1, yscale1, lim1, col1, False)
        finish(t)

    build(0, ha0, ha1)

    def pair(u, carry):
        build(2 * u + 1, hb0, hb1)
        one(2 * u, ha0, ha1)
        build(lax.rem(2 * u + 2, tiles), ha0, ha1)
        one(2 * u + 1, hb0, hb1)
        return carry

    lax.fori_loop(0, tiles // 2, pair, 0)

    working = q < nq - 1
    for col in (col0, col1):
        col[...] = jnp.where(working, col[...], -1.0)
    for c in copies[5:]:
        c.start()
    mine = jnp.where(working, jnp.maximum(out_ref[...], -1.0), -1.0)
    for c in copies[5:]:
        c.wait()
    out_ref[...] = jnp.maximum(mine, jnp.maximum(got0[...], got1[...]))


def constants():
    i = np.arange(L)
    suffix = (i[:, None] >= i[None, :]).astype(np.float32)
    prefix = (i[:, None] < i[None, :]).astype(np.float32)
    ones = np.concatenate([suffix, prefix, np.ones((L, L), np.float32)], axis=1)
    anti = np.eye(L, dtype=np.float32)[::-1]
    xmask = (i[None, :] >= i[:, None]).astype(np.float32)
    ymask = (i[None, :] <= i[:, None]).astype(np.float32)
    return [jnp.asarray(c, BF16) for c in (ones, anti, xmask, ymask)]


def per_device(series):
    rows = series.shape[0] // L
    tiles = rows // 4
    vm = pltpu.VMEM
    seq = vm((rows + 8, L), F32)
    cut = vm((16 * tiles, L), F32)
    sums = vm((16 * tiles, 3 * L), F32)
    line = vm((rows, L), F32)
    wide = vm((L, 11 * L), BF16)
    out = pl.pallas_call(
        kernel,
        out_shape=jax.ShapeDtypeStruct((rows, L), F32),
        in_specs=[pl.BlockSpec(memory_space=vm)] * 5,
        out_specs=pl.BlockSpec(memory_space=vm),
        scratch_shapes=[
            seq, seq, seq, seq, cut, cut, cut, sums, sums, sums,
            line, line, line, line, line, line, line, line,
            vm((tiles, L, 11 * L), BF16), vm((tiles, TILE, L), F32), vm((tiles, TILE, L), F32),
            wide, wide, wide, wide,
            vm((TILE, TILE), F32), vm((TILE, TILE), F32), vm((TILE, L), F32),
            line, line, line, line,
            pltpu.SemaphoreType.DMA((7,)), pltpu.SemaphoreType.DMA((7,)),
        ],
        compiler_params=pltpu.CompilerParams(
            collective_id=0, has_side_effects=True, vmem_limit_bytes=48 * 2**20
        ),
    )(series.reshape(rows, L), *constants())
    return out.reshape(-1)


def solution(mesh):
    placed = (P(("qry", "ref")),)
    return jax.shard_map(
        per_device, mesh=mesh, in_specs=placed, out_specs=P(("qry", "ref")), check_vma=False
    )
```

time: 658 us -> 46.9 us (0.07)
  the two profiles are of different devices: /device:TPU:24 before, /device:TPU:0 now
where the time goes in v1:
time: 46.9 us; the launch traced here: 46.5 us
  Pallas kernels  42 us (90%)
  local copies, waits for them, and re-layouts  4.51 us (10%)
    pallas_call x1, Pallas kernels, per_device(): pl.pallas_call(kernel, out_shape=jax.ShapeDtypeStruct((rows, L), F32), in...  42 us
    unnamed x11, local copies, waits for them, and re-layouts  4.51 us

profile of v1, /device:TPU:0, one launch (start us, length us, event | category | flops | bytes accessed | tf_op | source)
XLA Modules:
  0.0 46.5 jit_solution(10282295860680470537)
XLA Ops:
  0.0 0.0 copy-start
  0.0 0.9 %copy-done = bf16[128,384]{1,0:T(8,128)(2,1)S(1)} copy-done((bf16[128,384]{1,0:T(8,128)(2,1)S(1)}, bf16[128,384]{1,0:T(8,128)(2,1)}, u32[]{:S(2)}) %copy-start) | copy-done | bytes 98328
  0.9 0.0 copy-start.1
  0.9 0.8 %copy-done.1 = bf16[128,128]{1,0:T(8,128)(2,1)S(1)} copy-done((bf16[128,128]{1,0:T(8,128)(2,1)S(1)}, bf16[128,128]{1,0:T(8,128)(2,1)}, u32[]{:S(2)}) %copy-start.1) | copy-done | bytes 32792
  1.7 0.0 copy-start.2
  1.7 0.8 %copy-done.2 = bf16[128,128]{1,0:T(8,128)(2,1)S(1)} copy-done((bf16[128,128]{1,0:T(8,128)(2,1)S(1)}, bf16[128,128]{1,0:T(8,128)(2,1)}, u32[]{:S(2)}) %copy-start.2) | copy-done | bytes 32792
  2.4 0.0 copy-start.3
  2.4 0.8 %copy-done.3 = bf16[128,128]{1,0:T(8,128)(2,1)S(1)} copy-done((bf16[128,128]{1,0:T(8,128)(2,1)S(1)}, bf16[128,128]{1,0:T(8,128)(2,1)}, u32[]{:S(2)}) %copy-start.3) | copy-done | bytes 32792
  3.2 0.0 copy-start.4
  3.2 0.7 %copy-done.4 = f32[6144]{0:T(1024)S(1)} copy-done((f32[6144]{0:T(1024)S(1)}, f32[6144]{0:T(1024)}, u32[]{:S(2)}) %copy-start.4) | copy-done | bytes 24600
  3.9 42.0 %shard_map.55 = f32[48,128]{1,0:T(8,128)S(1)} custom-call(f32[48,128]{1,0:T(8,128)S(1)} %bitcast.3, bf16[128,384]{1,0:T(8,128)(2,1)S(1)} %copy-done, bf16[128,128]{1,0:T(8,128)(2,1)S(1)} %copy-done.3, bf16[128,128]{1,0:T(8,128)(2,1)S(1)} %copy-done.2, bf16[128,128]{1,0:T(8,128)(2,1)S(1)} %copy-done.1), custom_call_target="tpu_custom_call" | custom-call | tf_op jit(solution)/shard_map/pallas_call | solution.py:262
  45.9 0.6 %copy.7 = f32[6144]{0:T(1024)} copy(f32[6144]{0:T(1024)S(1)} %bitcast.2) | data formatting | bytes 49152
Async XLA Ops:
  0.0 0.9 %copy-start = (bf16[128,384]{1,0:T(8,128)(2,1)S(1)}, bf16[128,384]{1,0:T(8,128)(2,1)}, u32[]{:S(2)}) copy-start(bf16[128,384]{1,0:T(8,128)(2,1)} %constant.8.clone.ones) | copy-start | bytes 294916
  0.9 0.8 %copy-start.1 = (bf16[128,128]{1,0:T(8,128)(2,1)S(1)}, bf16[128,128]{1,0:T(8,128)(2,1)}, u32[]{:S(2)}) copy-start(bf16[128,128]{1,0:T(8,128)(2,1)} %constant.11.clone.ymask) | copy-start | bytes 98308
  1.7 0.8 %copy-start.2 = (bf16[128,128]{1,0:T(8,128)(2,1)S(1)}, bf16[128,128]{1,0:T(8,128)(2,1)}, u32[]{:S(2)}) copy-start(bf16[128,128]{1,0:T(8,128)(2,1)} %constant.10.clone.xmask) | copy-start | bytes 98308
  2.4 0.8 %copy-start.3 = (bf16[128,128]{1,0:T(8,128)(2,1)S(1)}, bf16[128,128]{1,0:T(8,128)(2,1)}, u32[]{:S(2)}) copy-start(bf16[128,128]{1,0:T(8,128)(2,1)} %constant.9.clone.anti) | copy-start | bytes 98308
  3.2 0.7 %copy-start.4 = (f32[6144]{0:T(1024)S(1)}, f32[6144]{0:T(1024)}, u32[]{:S(2)}) copy-start(f32[6144]{0:T(1024)} %param.5) | copy-start | bytes 73732

commit v2 on v1

--- a/solution.py
+++ b/solution.py
@@ -2,7 +2,6 @@
 
 import jax
 import jax.numpy as jnp
-import numpy as np
 from jax import lax
 from jax.experimental import pallas as pl
 from jax.experimental.pallas import tpu as pltpu
@@ -25,9 +24,10 @@
     return hi, mid, low
 
 
-def centre_tiles(src, dst, sums, tiles):
-    sums[...] = jnp.broadcast_to(jnp.sum(src[...], axis=1, keepdims=True), src.shape)
-    for t in range(tiles):
+def centre_tiles(src, dst, sums, lo, hi):
+    a, b = 8 * (lo // 2), 8 * ((4 * hi + 11) // 8)
+    sums[a:b] = jnp.broadcast_to(jnp.sum(src[a:b], axis=1, keepdims=True), (b - a, L))
+    for t in range(lo, hi):
         c = sums[4 * t + 4 : 4 * t + 5] + sums[4 * t + 5 : 4 * t + 6]
         c = c + (sums[4 * t + 6 : 4 * t + 7] + sums[4 * t + 7 : 4 * t + 8])
         c = c * (1.0 / TILE)
@@ -35,17 +35,18 @@
         dst[16 * t + 12 : 16 * t + 16] = jnp.zeros((4, L), F32)
 
 
-def window_stats(dst, ones, rb, r1, r2, total_row, scale_row, tiles):
-    v = dst[...]
+def window_stats(dst, ones, rb, r1, r2, total_row, scale_row, lo, hi):
+    part = slice(16 * lo, 16 * hi)
+    v = dst[part]
     w = ones[...]
-    hi, mid, low = split3(v)
+    hi_part, mid, low = split3(v)
     dot = functools.partial(jnp.dot, preferred_element_type=F32)
-    base = dot(hi, w)
-    rb[...] = base
-    r1[...] = base + (dot(mid, w) + dot(low, w))
+    base = dot(hi_part, w)
+    rb[part] = base
+    r1[part] = base + (dot(mid, w) + dot(low, w))
     q_hi, q_mid, q_low = split3(v * v)
-    r2[...] = dot(q_hi, w) + (dot(q_mid, w) + dot(q_low, w))
-    dst[...] = hi.astype(F32)
+    r2[part] = dot(q_hi, w) + (dot(q_mid, w) + dot(q_low, w))
+    dst[part] = hi_part.astype(F32)
 
     def window_sum(ref, t):
         b = 16 * t
@@ -55,7 +56,7 @@
             full = full + ref[b + r : b + r + 4, 2 * L : 3 * L]
         return s + full
 
-    for t in range(tiles):
+    for t in range(lo, hi):
         total_row[4 * t : 4 * t + 4] = window_sum(rb, t)
         mean = window_sum(r1, t) * (1.0 / M)
         power = window_sum(r2, t) * (1.0 / M)
@@ -77,11 +78,10 @@
 
 
 def kernel(
-    x_ref, ones, anti, xmask, ymask, out_ref,
-    xf, y0, y1, sums, xs, ys0, ys1, rb, r1, r2,
+    x_ref, out_ref, ones, anti, xmask, ymask, xf, y0, y1, sums, xs, ys0, ys1, rb, r1, r2,
     xtot, xscale, ytot0, yscale0, ytot1, yscale1, lim0, lim1,
     lx, mcol, fcol, ha0, ha1, hb0, hb1, s0, s1, racc, col0, col1, got0, got1,
-    send_sem, recv_sem,
+    send_sem, recv_sem, load_sem,
 ):
     tiles = x_ref.shape[0] // 4
     rows = x_ref.shape[0]
@@ -107,37 +107,100 @@
     before = at(me - 1)
     tail0 = at(nextq * nr + r + 1)
     tail1 = at(nextq * nr + nextr + 1)
-    sources = [after, (nextq, r), (nextq, nextr), tail0, tail1, (prevq, r), (prevq, prevr)]
+    back = wrap(before[0] - 1, nq)
+    working = q < nq - 1
+    inner = q >= 1
+    far = me - nr >= 1
+    takes0 = jnp.logical_and(working, me + nr + 1 < nq * nr)
+    takes1 = jnp.logical_and(working, jnp.logical_or(q < nq - 2, nextr < nr - 1))
+    gives = jnp.logical_and(me >= 1, before[0] < nq - 1)
+
     barrier = pltpu.get_barrier_semaphore()
-    for source in sources:
-        pl.semaphore_signal(barrier, inc=1, device_id=source, device_id_type=MESH)
-
-    back = wrap(before[0] - 1, nq)
+    for source, exists in (
+        (after, working), ((nextq, r), working), ((nextq, nextr), working),
+        (tail0, takes0), (tail1, takes1),
+    ):
+        @pl.when(exists)
+        def _():
+            pl.semaphore_signal(barrier, inc=1, device_id=source, device_id_type=MESH)
+
+    load = pltpu.make_async_copy(x_ref, xf.at[pl.ds(0, rows)], load_sem)
+    load.start()
     head = x_ref.at[pl.ds(0, 8)]
     plan = [
-        (head, xf.at[pl.ds(rows, 8)], before),
-        (x_ref, y0.at[pl.ds(0, rows)], (prevq, r)),
-        (x_ref, y1.at[pl.ds(0, rows)], (prevq, prevr)),
-        (head, y0.at[pl.ds(rows, 8)], (back, before[1])),
-        (head, y1.at[pl.ds(rows, 8)], (back, wrap(before[1] - 1, nr))),
-        (col0, got0, (nextq, r)),
-        (col1, got1, (nextq, nextr)),
+        (head, xf.at[pl.ds(rows, 8)], before, gives, working),
+        (x_ref, y0.at[pl.ds(0, rows)], (prevq, r), inner, working),
+        (x_ref, y1.at[pl.ds(0, rows)], (prevq, prevr), inner, working),
+        (head, y0.at[pl.ds(rows, 8)], (back, before[1]), far, takes0),
+        (head, y1.at[pl.ds(rows, 8)], (back, wrap(before[1] - 1, nr)), far, takes1),
+        (col0, got0, (nextq, r), working, inner),
+        (col1, got1, (nextq, nextr), working, inner),
     ]
     copies = [
         pltpu.make_async_remote_copy(
             src_ref=src, dst_ref=dst, send_sem=send_sem.at[n], recv_sem=recv_sem.at[n],
             device_id=device, device_id_type=MESH,
         )
-        for n, (src, dst, device) in enumerate(plan)
+        for n, (src, dst, device, _, _) in enumerate(plan)
     ]
-    pl.semaphore_wait(barrier, len(sources))
-    for c in copies[:5]:
-        c.start()
-    xf[0:rows, :] = x_ref[...]
-    copies[0].wait()
-    centre_tiles(xf, xs, sums, tiles)
-    window_stats(xs, ones, rb, r1, r2, xtot, xscale, tiles)
-    xs[...] = jnp.dot(xs[...].astype(BF16), anti[...], preferred_element_type=F32)
+    listeners = sum(jnp.where(p[3], 1, 0) for p in plan[:5])
+
+    @pl.when(listeners > 0)
+    def _():
+        pl.semaphore_wait(barrier, listeners)
+
+    for c, p in zip(copies[:5], plan):
+        pl.when(p[3])(c.start)
+
+    def arrived(n):
+        pl.when(plan[n][4])(copies[n].wait_recv)
+
+    i = lax.broadcasted_iota(jnp.int32, (L, L), 0)
+    j = lax.broadcasted_iota(jnp.int32, (L, L), 1)
+    flag = lambda c: jnp.where(c, 1.0, 0.0).astype(BF16)
+    ones[:, 0:L] = flag(i >= j)
+    ones[:, L : 2 * L] = flag(i < j)
+    ones[:, 2 * L : 3 * L] = jnp.ones((L, L), BF16)
+    anti[...] = flag(i + j == L - 1)
+    xmask[...] = flag(j >= i)
+    ymask[...] = flag(j <= i)
+    load.wait()
+
+    @pl.when(working)
+    def _():
+        compute(
+            arrived, (q, r, nq, nr, nextr, valid), out_ref, ones, anti, xmask, ymask,
+            xf, y0, y1, sums, xs, ys0, ys1, rb, r1, r2,
+            xtot, xscale, ytot0, yscale0, ytot1, yscale1, lim0, lim1,
+            lx, mcol, fcol, ha0, ha1, hb0, hb1, s0, s1, racc, col0, col1,
+        )
+
+    @pl.when(jnp.logical_not(working))
+    def _():
+        out_ref[...] = jnp.full((rows, L), -1.0, F32)
+
+    for n in (5, 6):
+        pl.when(plan[n][3])(copies[n].start)
+    for n in (5, 6):
+        arrived(n)
+
+        @pl.when(inner)
+        def _():
+            out_ref[...] = jnp.maximum(out_ref[...], (got0, got1)[n - 5][...])
+
+    for c, p in zip(copies, plan):
+        pl.when(p[3])(c.wait_send)
+
+
+def compute(
+    arrived, place, out_ref, ones, anti, xmask, ymask,
+    xf, y0, y1, sums, xs, ys0, ys1, rb, r1, r2,
+    xtot, xscale, ytot0, yscale0, ytot1, yscale1, lim0, lim1,
+    lx, mcol, fcol, ha0, ha1, hb0, hb1, s0, s1, racc, col0, col1,
+):
+    q, r, nq, nr, nextr, valid = place
+    rows = out_ref.shape[0]
+    tiles = rows // 4
 
     def prepare(t, carry):
         def put(out, g, m, v):
@@ -151,17 +214,37 @@
             fcol[t, L * i : L * i + L, :] = jnp.transpose(jnp.broadcast_to(scale, (L, L)))
         return carry
 
-    lax.fori_loop(0, tiles, prepare, 0)
-
-    for c in copies[1:5]:
-        c.wait()
+    early = tiles - 2
+
+    def query(lo, hi):
+        centre_tiles(xf, xs, sums, lo, hi)
+        window_stats(xs, ones, rb, r1, r2, xtot, xscale, lo, hi)
+        part = slice(16 * lo, 16 * hi)
+        xs[part] = jnp.dot(xs[part].astype(BF16), anti[...], preferred_element_type=F32)
+        lax.fori_loop(lo, hi, prepare, 0)
+
+    query(0, early)
+    arrived(0)
+    query(early, tiles)
+    zero = jnp.zeros((8, L), F32)
+
+    @pl.when(jnp.logical_and(q == nq - 2, r == nr - 1))
+    def _():
+        y0[rows : rows + 8] = zero
+
+    @pl.when(jnp.logical_and(q == nq - 2, nextr == nr - 1))
+    def _():
+        y1[rows : rows + 8] = zero
+
+    for n in range(1, 5):
+        arrived(n)
     cell = lax.broadcasted_iota(jnp.int32, (rows, L), 0) * L
     cell = cell + lax.broadcasted_iota(jnp.int32, (rows, L), 1)
     for y, ys, ytot, yscale, lim, place in (
         (y0, ys0, ytot0, yscale0, lim0, r), (y1, ys1, ytot1, yscale1, lim1, nextr)
     ):
-        centre_tiles(y, ys, sums, tiles)
-        window_stats(ys, ones, rb, r1, r2, ytot, yscale, tiles)
+        centre_tiles(y, ys, sums, 0, tiles)
+        window_stats(ys, ones, rb, r1, r2, ytot, yscale, 0, tiles)
         start = ((q + 1) * nr + place) * (rows * L)
         lim[...] = jnp.where(start + cell < valid, BIG, -BIG)
 
@@ -228,26 +311,7 @@
 
     lax.fori_loop(0, tiles // 2, pair, 0)
 
-    working = q < nq - 1
-    for col in (col0, col1):
-        col[...] = jnp.where(working, col[...], -1.0)
-    for c in copies[5:]:
-        c.start()
-    mine = jnp.where(working, jnp.maximum(out_ref[...], -1.0), -1.0)
-    for c in copies[5:]:
-        c.wait()
-    out_ref[...] = jnp.maximum(mine, jnp.maximum(got0[...], got1[...]))
-
-
-def constants():
-    i = np.arange(L)
-    suffix = (i[:, None] >= i[None, :]).astype(np.float32)
-    prefix = (i[:, None] < i[None, :]).astype(np.float32)
-    ones = np.concatenate([suffix, prefix, np.ones((L, L), np.float32)], axis=1)
-    anti = np.eye(L, dtype=np.float32)[::-1]
-    xmask = (i[None, :] >= i[:, None]).astype(np.float32)
-    ymask = (i[None, :] <= i[:, None]).astype(np.float32)
-    return [jnp.asarray(c, BF16) for c in (ones, anti, xmask, ymask)]
+    out_ref[...] = jnp.maximum(out_ref[...], -1.0)
 
 
 def per_device(series):
@@ -262,9 +326,10 @@
     out = pl.pallas_call(
         kernel,
         out_shape=jax.ShapeDtypeStruct((rows, L), F32),
-        in_specs=[pl.BlockSpec(memory_space=vm)] * 5,
+        in_specs=[pl.BlockSpec(memory_space=pltpu.HBM)],
         out_specs=pl.BlockSpec(memory_space=vm),
         scratch_shapes=[
+            vm((L, 3 * L), BF16), vm((L, L), BF16), vm((L, L), BF16), vm((L, L), BF16),
             seq, seq, seq, seq, cut, cut, cut, sums, sums, sums,
             line, line, line, line, line, line, line, line,
             vm((tiles, L, 11 * L), BF16), vm((tiles, TILE, L), F32), vm((tiles, TILE, L), F32),
@@ -272,11 +337,12 @@
             vm((TILE, TILE), F32), vm((TILE, TILE), F32), vm((TILE, L), F32),
             line, line, line, line,
             pltpu.SemaphoreType.DMA((7,)), pltpu.SemaphoreType.DMA((7,)),
+            pltpu.SemaphoreType.DMA,
         ],
         compiler_params=pltpu.CompilerParams(
             collective_id=0, has_side_effects=True, vmem_limit_bytes=48 * 2**20
         ),
-    )(series.reshape(rows, L), *constants())
+    )(series.reshape(rows, L))
     return out.reshape(-1)
 
 

time: 46.9 us -> 39 us (0.83)
  the two profiles are of different devices: /device:TPU:0 before, /device:TPU:24 now
where the time goes in v2:
time: 39 us; the launch traced here: 38.6 us
  Pallas kernels  37.2 us (95%)
  local copies, waits for them, and re-layouts  1.35 us (3%)
    pallas_call x1, Pallas kernels, per_device(): pl.pallas_call(kernel, out_shape=jax.ShapeDtypeStruct((rows, L), F32), in...  37.2 us
    unnamed x3, local copies, waits for them, and re-layouts  1.35 us

profile of v2, /device:TPU:24, one launch (start us, length us, event | category | flops | bytes accessed | tf_op | source)
XLA Modules:
  0.0 38.6 jit_solution(11119117517469726695)
XLA Ops:
  0.0 0.0 copy-start
  0.0 0.7 %copy-done = f32[6144]{0:T(1024)S(1)} copy-done((f32[6144]{0:T(1024)S(1)}, f32[6144]{0:T(1024)}, u32[]{:S(2)}) %copy-start) | copy-done | bytes 24600
  0.7 37.2 %shard_map.17 = f32[48,128]{1,0:T(8,128)S(1)} custom-call(f32[48,128]{1,0:T(8,128)S(1)} %bitcast.3), custom_call_target="tpu_custom_call" | custom-call | tf_op jit(solution)/shard_map/pallas_call | solution.py:326
  37.9 0.6 %copy.3 = f32[6144]{0:T(1024)} copy(f32[6144]{0:T(1024)S(1)} %bitcast.2) | data formatting | bytes 49152
Async XLA Ops:
  0.0 0.7 %copy-start = (f32[6144]{0:T(1024)S(1)}, f32[6144]{0:T(1024)}, u32[]{:S(2)}) copy-start(f32[6144]{0:T(1024)} %param.1) | copy-start | bytes 73732

commit v3 on v2

v3 whole, which is shorter than its diff:
```python
import functools

import jax
import jax.numpy as jnp
from jax import lax
from jax.experimental import pallas as pl
from jax.experimental.pallas import tpu as pltpu
from jax.sharding import PartitionSpec as P

M = 1024
TILE = 512
L = 128
F32 = jnp.float32
BF16 = jnp.bfloat16
MESH = pl.DeviceIdType.MESH
BIG = 1e30


def split3(v):
    hi = v.astype(BF16)
    rest = v - hi.astype(F32)
    mid = rest.astype(BF16)
    low = (rest - mid.astype(F32)).astype(BF16)
    return hi, mid, low


def centre_tiles(src, dst, sums, lo, hi):
    a, b = 8 * (lo // 2), 8 * ((4 * hi + 11) // 8)
    sums[a:b] = jnp.broadcast_to(jnp.sum(src[a:b], axis=1, keepdims=True), (b - a, L))
    for t in range(lo, hi):
        c = sums[4 * t + 4 : 4 * t + 5] + sums[4 * t + 5 : 4 * t + 6]
        c = c + (sums[4 * t + 6 : 4 * t + 7] + sums[4 * t + 7 : 4 * t + 8])
        c = c * (1.0 / TILE)
        dst[16 * t : 16 * t + 12] = src[4 * t : 4 * t + 12] - c
        dst[16 * t + 12 : 16 * t + 16] = jnp.zeros((4, L), F32)


def window_stats(dst, ones, rb, r1, r2, total_row, scale_row, lo, hi):
    part = slice(16 * lo, 16 * hi)
    v = dst[part]
    w = ones[...]
    hi_part, mid, low = split3(v)
    dot = functools.partial(jnp.dot, preferred_element_type=F32)
    base = dot(hi_part, w)
    rb[part] = base
    r1[part] = base + (dot(mid, w) + dot(low, w))
    q_hi, q_mid, q_low = split3(v * v)
    r2[part] = dot(q_hi, w) + (dot(q_mid, w) + dot(q_low, w))
    dst[part] = hi_part.astype(F32)

    def window_sum(ref, t):
        b = 16 * t
        s = ref[b : b + 4, 0:L] + ref[b + 8 : b + 12, L : 2 * L]
        full = ref[b + 1 : b + 5, 2 * L : 3 * L]
        for r in range(2, 8):
            full = full + ref[b + r : b + r + 4, 2 * L : 3 * L]
        return s + full

    for t in range(lo, hi):
        total_row[4 * t : 4 * t + 4] = window_sum(rb, t)
        mean = window_sum(r1, t) * (1.0 / M)
        power = window_sum(r2, t) * (1.0 / M)
        spread = jnp.maximum(power - mean * mean, 0.0)
        scale_row[4 * t : 4 * t + 4] = lax.rsqrt(spread + 1e-05) * (1.0 / M**0.5)


def turned(rows, base, which, first, g):
    return [
        pltpu.roll(
            jnp.broadcast_to(rows[pl.ds(base + m, 1), :], (16, L)).astype(BF16),
            (first + 16 * g) % L, 1, stride=1, stride_axis=0,
        )
        for m in which
    ]


def own_blocks(rows, t, masks, lhs_even, lhs_odd):
    none = jnp.zeros((16, L), BF16)
    for g in range(8):
        mask = masks[16 * g : 16 * g + 16, :] > 0
        r0, r1, r2, r3, r8, r9, r10, r11 = turned(rows, 16 * t, (0, 1, 2, 3, 8, 9, 10, 11), 0, g)
        pick = lambda u, v: jnp.where(mask, u, v)
        left1, left3 = pick(r1, none), pick(r3, none)
        right7, right9 = pick(none, r8), pick(none, r10)
        for half, even, odd in (
            (0, (pick(r0, r1), right7, left1), (left1, pick(r8, r9), right7)),
            (1, (pick(r2, r3), right9, left3), (left3, pick(r10, r11), right9)),
        ):
            part = slice(L * half + 16 * g, L * half + 16 * g + 16)
            for k in range(3):
                lhs_even[t, part, L * k : L * k + L] = even[k]
                lhs_odd[t, part, L * k : L * k + L] = odd[k]


def shear(rows, base, out, masks):
    for g in range(8):
        mask = masks[16 * g : 16 * g + 16, :] > 0
        turns = turned(rows, base, range(12), 1, g)
        for m in range(11):
            out[16 * g : 16 * g + 16, L * m : L * m + L] = jnp.where(mask, turns[m], turns[m + 1])


def kernel(
    x_ref, out_ref, ones, anti, xmask, ymask, xf, y0, y1, sums, xs, ys0, ys1, rb, r1, r2,
    xtot, xscale, ytot0, yscale0, ytot1, yscale1,
    lhs_even, lhs_odd, fcol, ha0, ha1, hb0, hb1, na0, na1, nb0, nb1, se0, se1, so0, so1, sz0, sz1, racc, col0, col1, got0, got1,
    send_sem, recv_sem, load_sem,
):
    tiles = x_ref.shape[0] // 4
    rows = x_ref.shape[0]
    q = lax.axis_index("qry")
    r = lax.axis_index("ref")
    nq = lax.axis_size("qry")
    nr = lax.axis_size("ref")
    valid = nq * nr * rows * L - M + 1

    def wrap(a, n):
        return lax.rem(a + 2 * n, n)

    def at(flat):
        flat = lax.rem(flat + nq * nr, nq * nr)
        return flat // nr, lax.rem(flat, nr)

    me = q * nr + r
    nextq = wrap(q + 1, nq)
    nextr = wrap(r + 1, nr)
    prevq = wrap(q - 1, nq)
    prevr = wrap(r - 1, nr)
    after = at(me + 1)
    before = at(me - 1)
    behind = at(me - nr + 1)
    ahead = at(me + nr - 1)
    working = q >= 1
    above = q < nq - 1
    tailed = jnp.logical_and(working, me < nq * nr - 1)
    far = me >= nr + 1
    gives = jnp.logical_and(me >= 1, me <= nq * nr - nr)

    barrier = pltpu.get_barrier_semaphore()
    for source, exists in (
        (after, tailed), ((prevq, r), working), ((prevq, prevr), working), (behind, working),
    ):
        @pl.when(exists)
        def _():
            pl.semaphore_signal(barrier, inc=1, device_id=source, device_id_type=MESH)

    load = pltpu.make_async_copy(x_ref, xf.at[pl.ds(0, rows)], load_sem)
    load.start()
    head = x_ref.at[pl.ds(0, 8)]
    plan = [
        (head, xf.at[pl.ds(rows, 8)], before, far, tailed),
        (x_ref, y0.at[pl.ds(0, rows)], (nextq, r), above, working),
        (x_ref, y1.at[pl.ds(0, rows)], (nextq, nextr), above, working),
        (head, y0.at[pl.ds(rows, 8)], ahead, gives, working),
        (col0, got0, (prevq, r), working, above),
        (col1, got1, (prevq, prevr), working, above),
    ]
    copies = [
        pltpu.make_async_remote_copy(
            src_ref=src, dst_ref=dst, send_sem=send_sem.at[n], recv_sem=recv_sem.at[n],
            device_id=device, device_id_type=MESH,
        )
        for n, (src, dst, device, _, _) in enumerate(plan)
    ]
    listeners = sum(jnp.where(p[3], 1, 0) for p in plan[:4])

    @pl.when(listeners > 0)
    def _():
        pl.semaphore_wait(barrier, listeners)

    for c, p in zip(copies[:4], plan):
        pl.when(p[3])(c.start)

    def arrived(n):
        pl.when(plan[n][4])(copies[n].wait_recv)

    i = lax.broadcasted_iota(jnp.int32, (L, L), 0)
    j = lax.broadcasted_iota(jnp.int32, (L, L), 1)
    flag = lambda c: jnp.where(c, 1.0, 0.0).astype(BF16)
    ones[:, 0:L] = flag(i >= j)
    ones[:, L : 2 * L] = flag(i < j)
    ones[:, 2 * L : 3 * L] = jnp.ones((L, L), BF16)
    anti[...] = flag(i + j == L - 1)
    xmask[...] = flag(j >= i)
    ymask[...] = flag(j <= i)
    load.wait()

    @pl.when(working)
    def _():
        compute(
            arrived, (me, r, nq * nr, valid), out_ref, ones, anti, xmask, ymask,
            xf, y0, y1, sums, xs, ys0, ys1, rb, r1, r2,
            xtot, xscale, ytot0, yscale0, ytot1, yscale1,
            lhs_even, lhs_odd, fcol, ha0, ha1, hb0, hb1, na0, na1, nb0, nb1, se0, se1, so0, so1, sz0, sz1, racc, col0, col1,
        )

    @pl.when(jnp.logical_not(working))
    def _():
        out_ref[...] = jnp.full((rows, L), -1.0, F32)

    for n in (4, 5):
        pl.when(plan[n][3])(copies[n].start)
    for n in (4, 5):
        arrived(n)

        @pl.when(above)
        def _():
            out_ref[...] = jnp.maximum(out_ref[...], (got0, got1)[n - 4][...])

    for c, p in zip(copies, plan):
        pl.when(p[3])(c.wait_send)


def compute(
    arrived, place, out_ref, ones, anti, xmask, ymask,
    xf, y0, y1, sums, xs, ys0, ys1, rb, r1, r2,
    xtot, xscale, ytot0, yscale0, ytot1, yscale1,
    lhs_even, lhs_odd, fcol, ha0, ha1, hb0, hb1, na0, na1, nb0, nb1, se0, se1, so0, so1, sz0, sz1, racc, col0, col1,
):
    me, r, count, valid = place
    rows = out_ref.shape[0]
    tiles = rows // 4

    slot = lax.broadcasted_iota(jnp.int32, (8, L), 0)
    lane = lax.broadcasted_iota(jnp.int32, (8, L), 1)
    parts = lambda v: [p.astype(F32) for p in split3(v)]

    def prepare(t, carry):
        own_blocks(xs, t, xmask, lhs_even, lhs_odd)
        for i in range(4):
            mean = jnp.broadcast_to(xtot[pl.ds(4 * t + i, 1), :] * (-1.0 / M), (8, L))
            hi, mid, low = parts(mean)
            window = me * (rows * L) + TILE * t + L * i + lane
            bias = jnp.where(jnp.logical_and(slot == 6, window >= valid), -BIG, 0.0)
            cols = jnp.where(slot < 3, hi, jnp.where(slot < 5, mid, jnp.where(slot < 6, low, bias)))
            cols = jnp.transpose(jnp.concatenate([cols, jnp.zeros((L - 8, L), F32)], axis=0))
            lhs = lhs_odd if i % 2 else lhs_even
            lhs[t, L * (i // 2) : L * (i // 2) + L, 3 * L : 4 * L] = cols.astype(BF16)
            scale = xscale[pl.ds(4 * t + i, 1), :]
            fcol[t, L * i : L * i + L, :] = jnp.transpose(jnp.broadcast_to(scale, (L, L)))
        middle = xs[pl.ds(16 * t + 2, 8), :]
        empty = jnp.zeros((8, L), F32)
        first = jnp.concatenate([middle, empty], axis=0).astype(BF16)
        second = jnp.concatenate([empty, middle], axis=0).astype(BF16)
        none = jnp.zeros((16, L), BF16)
        for k, v in enumerate((first, second, none, none)):
            lhs_even[t, 256:272, L * k : L * k + L] = v
        for k, v in enumerate((none, none, first, none)):
            lhs_even[t, 272:288, L * k : L * k + L] = v
            lhs_odd[t, 256:272, L * k : L * k + L] = v
        return carry

    early = tiles - 2

    def query(lo, hi):
        centre_tiles(xf, xs, sums, lo, hi)
        window_stats(xs, ones, rb, r1, r2, xtot, xscale, lo, hi)
        part = slice(16 * lo, 16 * hi)
        xs[part] = jnp.dot(xs[part].astype(BF16), anti[...], preferred_element_type=F32)
        lax.fori_loop(lo, hi, prepare, 0)

    query(0, early)
    arrived(0)

    @pl.when(me == count - 1)
    def _():
        xf[rows : rows + 8] = jnp.zeros((8, L), F32)

    query(early, tiles)
    for n in range(1, 4):
        arrived(n)
    y1[rows : rows + 8] = jnp.where(r >= 1, y0[0:8], xf[0:8])
    for y, ys, ytot, yscale in ((y0, ys0, ytot0, yscale0), (y1, ys1, ytot1, yscale1)):
        centre_tiles(y, ys, sums, 0, tiles)
        window_stats(ys, ones, rb, r1, r2, ytot, yscale, 0, tiles)

    for ref in (na0, na1, nb0, nb1):
        ref[...] = jnp.zeros((L, TILE), BF16)

    def build(t, h0, h1, n0, n1):
        for ys, ytot, h, n in ((ys0, ytot0, h0, n0), (ys1, ytot1, h1, n1)):
            shear(ys, 16 * t, h, ymask)
            for j in range(4):
                hi, mid, low = parts(jnp.broadcast_to(ytot[pl.ds(4 * t + j, 1), :], (8, L)))
                v = jnp.where(slot == 1, mid, jnp.where(slot == 2, low, jnp.where(slot == 4, mid, hi)))
                v = jnp.where(slot < 6, v, jnp.where(slot == 6, 1.0, 0.0))
                v = jnp.concatenate([v, jnp.zeros((8, L), F32)], axis=0)
                n[0:16, L * j : L * j + L] = v.astype(BF16)

    def products(t, h, n, se, so, sz):
        dot = functools.partial(jnp.dot, preferred_element_type=F32)
        block = lambda k: h[:, L * k : L * k + TILE]
        last = n[...]
        se[...] = dot(lhs_even[t], jnp.concatenate([block(0), block(7), block(1), last], axis=0))
        so[...] = dot(lhs_odd[t], jnp.concatenate([block(0), block(7), block(6), last], axis=0))
        sz[...] = dot(lhs_even[t, 256:272, 0:L], h[:, 5 * L : 6 * L])

    def maxima(t, se, so, sz, yscale, col, first):
        scale = [jnp.broadcast_to(yscale[pl.ds(4 * t + j, 1), :], (8, L)) for j in range(4)]

        def middle(row, m):
            if m < 4:
                v = se[256 + row : 257 + row, L * m : L * m + L]
            elif m == 4:
                v = se[272 + row : 273 + row, 3 * L : 4 * L]
            elif m == 5:
                v = sz[row : row + 1, :]
            elif m == 6:
                v = so[256 + row : 257 + row, 0:L]
            else:
                v = se[264 + row : 265 + row, L * (m - 7) : L * (m - 7) + L]
            return jnp.broadcast_to(v, (8, L))

        best = [None] * 4
        for half in range(2):
            shared = []
            for e in range(-2, 4):
                v = [middle(2 * half + k - 2, k + e) for k in range(2, 8)]
                shared.append((v[0] + v[1]) + (v[2] + v[3]) + (v[4] + v[5]))
            for g in range(16):
                turn = [pltpu.roll(c, 8 * g, 1, stride=1, stride_axis=0) for c in shared]
                mask = lane >= slot + 8 * g
                slid = [jnp.where(mask, turn[e + 1], turn[e]) for e in range(5)]
                for odd, s in ((0, se), (1, so)):
                    part = pl.ds(L * half + 8 * g, 8)
                    place = pl.ds(L * (2 * half + odd) + 8 * g, 8)
                    factor = fcol[t, place, :]
                    row = None if first else racc[place, :]
                    for j in range(4):
                        v = s[part, L * j : L * j + L] + slid[j - odd + 1]
                        a = v * scale[j]
                        row = a if row is None else jnp.maximum(row, a)
                        b = v * factor
                        best[j] = b if best[j] is None else jnp.maximum(best[j], b)
                    racc[place, :] = row
        for j in range(4):
            top = jnp.max(best[j], axis=0, keepdims=True)
            col[pl.ds(4 * t + j, 1), :] = jnp.maximum(top * yscale[pl.ds(4 * t + j, 1), :], -1.0)

    def finish(t):
        for i in range(4):
            top = jnp.max(jnp.transpose(racc[L * i : L * i + L, :]), axis=0, keepdims=True)
            out_ref[pl.ds(4 * t + i, 1), :] = top * xscale[pl.ds(4 * t + i, 1), :]

    def one(t, h0, h1, n0, n1):
        products(t, h0, n0, se0, so0, sz0)
        products(t, h1, n1, se1, so1, sz1)
        maxima(t, se0, so0, sz0, yscale0, col0, True)
        maxima(t, se1, so1, sz1, yscale1, col1, False)
        finish(t)

    build(0, ha0, ha1, na0, na1)

    def pair(u, carry):
        build(2 * u + 1, hb0, hb1, nb0, nb1)
        one(2 * u, ha0, ha1, na0, na1)
        build(lax.rem(2 * u + 2, tiles), ha0, ha1, na0, na1)
        one(2 * u + 1, hb0, hb1, nb0, nb1)
        return carry

    lax.fori_loop(0, tiles // 2, pair, 0)

    cell = lax.broadcasted_iota(jnp.int32, (rows, L), 0) * L
    cell = cell + lax.broadcasted_iota(jnp.int32, (rows, L), 1)
    keep = me * (rows * L) + cell < valid
    out_ref[...] = jnp.where(keep, jnp.maximum(out_ref[...], -1.0), -1.0)


def per_device(series):
    rows = series.shape[0] // L
    tiles = rows // 4
    vm = pltpu.VMEM
    seq = vm((rows + 8, L), F32)
    cut = vm((16 * tiles, L), F32)
    sums = vm((16 * tiles, 3 * L), F32)
    line = vm((rows, L), F32)
    wide = vm((L, 11 * L), BF16)
    slots = vm((L, TILE), BF16)
    out = pl.pallas_call(
        kernel,
        out_shape=jax.ShapeDtypeStruct((rows, L), F32),
        in_specs=[pl.BlockSpec(memory_space=pltpu.HBM)],
        out_specs=pl.BlockSpec(memory_space=vm),
        scratch_shapes=[
            vm((L, 3 * L), BF16), vm((L, L), BF16), vm((L, L), BF16), vm((L, L), BF16),
            seq, seq, seq, seq, cut, cut, cut, sums, sums, sums,
            line, line, line, line, line, line,
            vm((tiles, 288, TILE), BF16), vm((tiles, 272, TILE), BF16), vm((tiles, TILE, L), F32),
            wide, wide, wide, wide, slots, slots, slots, slots,
            vm((288, TILE), F32), vm((288, TILE), F32), vm((272, TILE), F32), vm((272, TILE), F32),
            vm((16, L), F32), vm((16, L), F32), vm((TILE, L), F32),
            line, line, line, line,
            pltpu.SemaphoreType.DMA((6,)), pltpu.SemaphoreType.DMA((6,)),
            pltpu.SemaphoreType.DMA,
        ],
        compiler_params=pltpu.CompilerParams(
            collective_id=0, has_side_effects=True, vmem_limit_bytes=48 * 2**20
        ),
    )(series.reshape(rows, L))
    return out.reshape(-1)


def solution(mesh):
    placed = (P(("qry", "ref")),)
    return jax.shard_map(
        per_device, mesh=mesh, in_specs=placed, out_specs=P(("qry", "ref")), check_vma=False
    )
```

time: 39 us -> 31.4 us (0.81)
  the two profiles are of different devices: /device:TPU:24 before, /device:TPU:1 now
where the time goes in v3:
time: 31.4 us; the launch traced here: 31.2 us
  Pallas kernels  29.9 us (95%)
  local copies, waits for them, and re-layouts  1.35 us (4%)
    pallas_call x1, Pallas kernels, per_device(): pl.pallas_call(kernel, out_shape=jax.ShapeDtypeStruct((rows, L), F32), in...  29.9 us
    unnamed x3, local copies, waits for them, and re-layouts  1.35 us

profile of v3, /device:TPU:1, one launch (start us, length us, event | category | flops | bytes accessed | tf_op | source)
XLA Modules:
  0.0 31.2 jit_solution(8016185394646509785)
XLA Ops:
  0.0 0.0 copy-start
  0.0 0.7 %copy-done = f32[6144]{0:T(1024)S(1)} copy-done((f32[6144]{0:T(1024)S(1)}, f32[6144]{0:T(1024)}, u32[]{:S(2)}) %copy-start) | copy-done | bytes 24600
  0.7 29.9 %shard_map.17 = f32[48,128]{1,0:T(8,128)S(1)} custom-call(f32[48,128]{1,0:T(8,128)S(1)} %bitcast.3), custom_call_target="tpu_custom_call" | custom-call | tf_op jit(solution)/shard_map/pallas_call | solution.py:379
  30.6 0.6 %copy.3 = f32[6144]{0:T(1024)} copy(f32[6144]{0:T(1024)S(1)} %bitcast.2) | data formatting | bytes 49152
Async XLA Ops:
  0.0 0.7 %copy-start = (f32[6144]{0:T(1024)S(1)}, f32[6144]{0:T(1024)}, u32[]{:S(2)}) copy-start(f32[6144]{0:T(1024)} %param.1) | copy-start | bytes 73732

commit v4 on v3

--- a/solution.py
+++ b/solution.py
@@ -14,6 +14,7 @@
 BF16 = jnp.bfloat16
 MESH = pl.DeviceIdType.MESH
 BIG = 1e30
+GROUP = 4
 
 
 def split3(v):
@@ -92,8 +93,8 @@
                 lhs_odd[t, part, L * k : L * k + L] = odd[k]
 
 
-def shear(rows, base, out, masks):
-    for g in range(8):
+def shear(rows, base, out, masks, groups):
+    for g in groups:
         mask = masks[16 * g : 16 * g + 16, :] > 0
         turns = turned(rows, base, range(12), 1, g)
         for m in range(11):
@@ -103,7 +104,7 @@
 def kernel(
     x_ref, out_ref, ones, anti, xmask, ymask, xf, y0, y1, sums, xs, ys0, ys1, rb, r1, r2,
     xtot, xscale, ytot0, yscale0, ytot1, yscale1,
-    lhs_even, lhs_odd, fcol, ha0, ha1, hb0, hb1, na0, na1, nb0, nb1, se0, se1, so0, so1, sz0, sz1, racc, col0, col1, got0, got1,
+    lhs_even, lhs_odd, fcol, ha0, ha1, hb0, hb1, na0, na1, nb0, nb1, se0, se1, so0, so1, sz0, sz1, racc0, racc1, racc2, racc3, col0, col1, got0, got1,
     send_sem, recv_sem, load_sem,
 ):
     tiles = x_ref.shape[0] // 4
@@ -174,6 +175,14 @@
     def arrived(n):
         pl.when(plan[n][4])(copies[n].wait_recv)
 
+    def give(t, several, n):
+        part = pl.ds(pl.multiple_of(4 * t, 8), 4 * several)
+        src, dst, device = plan[n][:3]
+        pltpu.make_async_remote_copy(
+            src_ref=src.at[part], dst_ref=dst.at[part], send_sem=send_sem.at[n],
+            recv_sem=recv_sem.at[n], device_id=device, device_id_type=MESH,
+        ).start()
+
     i = lax.broadcasted_iota(jnp.int32, (L, L), 0)
     j = lax.broadcasted_iota(jnp.int32, (L, L), 1)
     flag = lambda c: jnp.where(c, 1.0, 0.0).astype(BF16)
@@ -188,10 +197,10 @@
     @pl.when(working)
     def _():
         compute(
-            arrived, (me, r, nq * nr, valid), out_ref, ones, anti, xmask, ymask,
+            arrived, give, (me, r, nq * nr, valid), out_ref, ones, anti, xmask, ymask,
             xf, y0, y1, sums, xs, ys0, ys1, rb, r1, r2,
             xtot, xscale, ytot0, yscale0, ytot1, yscale1,
-            lhs_even, lhs_odd, fcol, ha0, ha1, hb0, hb1, na0, na1, nb0, nb1, se0, se1, so0, so1, sz0, sz1, racc, col0, col1,
+            lhs_even, lhs_odd, fcol, ha0, ha1, hb0, hb1, na0, na1, nb0, nb1, se0, se1, so0, so1, sz0, sz1, racc0, racc1, racc2, racc3, col0, col1,
         )
 
     @pl.when(jnp.logical_not(working))
@@ -199,8 +208,6 @@
         out_ref[...] = jnp.full((rows, L), -1.0, F32)
 
     for n in (4, 5):
-        pl.when(plan[n][3])(copies[n].start)
-    for n in (4, 5):
         arrived(n)
 
         @pl.when(above)
@@ -212,10 +219,10 @@
 
 
 def compute(
-    arrived, place, out_ref, ones, anti, xmask, ymask,
+    arrived, give, place, out_ref, ones, anti, xmask, ymask,
     xf, y0, y1, sums, xs, ys0, ys1, rb, r1, r2,
     xtot, xscale, ytot0, yscale0, ytot1, yscale1,
-    lhs_even, lhs_odd, fcol, ha0, ha1, hb0, hb1, na0, na1, nb0, nb1, se0, se1, so0, so1, sz0, sz1, racc, col0, col1,
+    lhs_even, lhs_odd, fcol, ha0, ha1, hb0, hb1, na0, na1, nb0, nb1, se0, se1, so0, so1, sz0, sz1, racc0, racc1, racc2, racc3, col0, col1,
 ):
     me, r, count, valid = place
     rows = out_ref.shape[0]
@@ -260,13 +267,6 @@
         lax.fori_loop(lo, hi, prepare, 0)
 
     query(0, early)
-    arrived(0)
-
-    @pl.when(me == count - 1)
-    def _():
-        xf[rows : rows + 8] = jnp.zeros((8, L), F32)
-
-    query(early, tiles)
     for n in range(1, 4):
         arrived(n)
     y1[rows : rows + 8] = jnp.where(r >= 1, y0[0:8], xf[0:8])
@@ -277,89 +277,157 @@
     for ref in (na0, na1, nb0, nb1):
         ref[...] = jnp.zeros((L, TILE), BF16)
 
-    def build(t, h0, h1, n0, n1):
-        for ys, ytot, h, n in ((ys0, ytot0, h0, n0), (ys1, ytot1, h1, n1)):
-            shear(ys, 16 * t, h, ymask)
-            for j in range(4):
-                hi, mid, low = parts(jnp.broadcast_to(ytot[pl.ds(4 * t + j, 1), :], (8, L)))
-                v = jnp.where(slot == 1, mid, jnp.where(slot == 2, low, jnp.where(slot == 4, mid, hi)))
-                v = jnp.where(slot < 6, v, jnp.where(slot == 6, 1.0, 0.0))
-                v = jnp.concatenate([v, jnp.zeros((8, L), F32)], axis=0)
-                n[0:16, L * j : L * j + L] = v.astype(BF16)
-
-    def products(t, h, n, se, so, sz):
+    def build(job, quarter):
+        t, ys, ytot, h, n = job
+        shear(ys, 16 * t, h, ymask, (2 * quarter, 2 * quarter + 1))
+        j = quarter
+        hi, mid, low = parts(jnp.broadcast_to(ytot[pl.ds(4 * t + j, 1), :], (8, L)))
+        v = jnp.where(slot == 1, mid, jnp.where(slot == 2, low, jnp.where(slot == 4, mid, hi)))
+        v = jnp.where(slot < 6, v, jnp.where(slot == 6, 1.0, 0.0))
+        v = jnp.concatenate([v, jnp.zeros((8, L), F32)], axis=0)
+        n[0:16, L * j : L * j + L] = v.astype(BF16)
+
+    def products(job, odd):
+        t, h, n, (se, so, sz) = job
         dot = functools.partial(jnp.dot, preferred_element_type=F32)
         block = lambda k: h[:, L * k : L * k + TILE]
         last = n[...]
-        se[...] = dot(lhs_even[t], jnp.concatenate([block(0), block(7), block(1), last], axis=0))
-        so[...] = dot(lhs_odd[t], jnp.concatenate([block(0), block(7), block(6), last], axis=0))
-        sz[...] = dot(lhs_even[t, 256:272, 0:L], h[:, 5 * L : 6 * L])
-
-    def maxima(t, se, so, sz, yscale, col, first):
-        scale = [jnp.broadcast_to(yscale[pl.ds(4 * t + j, 1), :], (8, L)) for j in range(4)]
-
-        def middle(row, m):
-            if m < 4:
-                v = se[256 + row : 257 + row, L * m : L * m + L]
-            elif m == 4:
-                v = se[272 + row : 273 + row, 3 * L : 4 * L]
-            elif m == 5:
-                v = sz[row : row + 1, :]
-            elif m == 6:
-                v = so[256 + row : 257 + row, 0:L]
-            else:
-                v = se[264 + row : 265 + row, L * (m - 7) : L * (m - 7) + L]
-            return jnp.broadcast_to(v, (8, L))
-
-        best = [None] * 4
-        for half in range(2):
+        if odd:
+            so[...] = dot(lhs_odd[t], jnp.concatenate([block(0), block(7), block(6), last], axis=0))
+        else:
+            se[...] = dot(lhs_even[t], jnp.concatenate([block(0), block(7), block(1), last], axis=0))
+            sz[...] = dot(lhs_even[t, 256:272, 0:L], h[:, 5 * L : 6 * L])
+
+    def middle(sums, row, m):
+        se, so, sz = sums
+        if m < 4:
+            v = se[256 + row : 257 + row, L * m : L * m + L]
+        elif m == 4:
+            v = se[272 + row : 273 + row, 3 * L : 4 * L]
+        elif m == 5:
+            v = sz[row : row + 1, :]
+        elif m == 6:
+            v = so[256 + row : 257 + row, 0:L]
+        else:
+            v = se[264 + row : 265 + row, L * (m - 7) : L * (m - 7) + L]
+        return jnp.broadcast_to(v, (8, L))
+
+    def maxima(job, half, state, groups):
+        t, sums, yscale, col, racc, first = job
+        if "scale" not in state:
+            state["scale"] = [
+                jnp.broadcast_to(yscale[pl.ds(4 * t + j, 1), :], (8, L)) for j in range(4)
+            ]
+            state["best"] = [None] * 4
+        scale, best = state["scale"], state["best"]
+        if ("shared", half) not in state:
             shared = []
             for e in range(-2, 4):
-                v = [middle(2 * half + k - 2, k + e) for k in range(2, 8)]
+                v = [middle(sums, 2 * half + k - 2, k + e) for k in range(2, 8)]
                 shared.append((v[0] + v[1]) + (v[2] + v[3]) + (v[4] + v[5]))
-            for g in range(16):
-                turn = [pltpu.roll(c, 8 * g, 1, stride=1, stride_axis=0) for c in shared]
-                mask = lane >= slot + 8 * g
-                slid = [jnp.where(mask, turn[e + 1], turn[e]) for e in range(5)]
-                for odd, s in ((0, se), (1, so)):
-                    part = pl.ds(L * half + 8 * g, 8)
-                    place = pl.ds(L * (2 * half + odd) + 8 * g, 8)
-                    factor = fcol[t, place, :]
-                    row = None if first else racc[place, :]
-                    for j in range(4):
-                        v = s[part, L * j : L * j + L] + slid[j - odd + 1]
-                        a = v * scale[j]
-                        row = a if row is None else jnp.maximum(row, a)
-                        b = v * factor
-                        best[j] = b if best[j] is None else jnp.maximum(best[j], b)
-                    racc[place, :] = row
+            state["shared", half] = shared
+        shared = state["shared", half]
+        for g in groups:
+            turn = [pltpu.roll(c, 8 * g, 1, stride=1, stride_axis=0) for c in shared]
+            mask = lane >= slot + 8 * g
+            slid = [jnp.where(mask, turn[e + 1], turn[e]) for e in range(5)]
+            for odd, s in ((0, sums[0]), (1, sums[1])):
+                part = pl.ds(L * half + 8 * g, 8)
+                place = pl.ds(L * (2 * half + odd) + 8 * g, 8)
+                factor = fcol[t, place, :]
+                row = None if first else racc[place, :]
+                for j in range(4):
+                    v = s[part, L * j : L * j + L] + slid[j - odd + 1]
+                    a = v * scale[j]
+                    row = a if row is None else jnp.maximum(row, a)
+                    b = v * factor
+                    best[j] = b if best[j] is None else jnp.maximum(best[j], b)
+                racc[place, :] = row
+
+    def close(job, state):
+        t, _, yscale, col, _, _ = job
         for j in range(4):
-            top = jnp.max(best[j], axis=0, keepdims=True)
+            top = jnp.max(state["best"][j], axis=0, keepdims=True)
             col[pl.ds(4 * t + j, 1), :] = jnp.maximum(top * yscale[pl.ds(4 * t + j, 1), :], -1.0)
 
-    def finish(t):
-        for i in range(4):
-            top = jnp.max(jnp.transpose(racc[L * i : L * i + L, :]), axis=0, keepdims=True)
-            out_ref[pl.ds(4 * t + i, 1), :] = top * xscale[pl.ds(4 * t + i, 1), :]
-
-    def one(t, h0, h1, n0, n1):
-        products(t, h0, n0, se0, so0, sz0)
-        products(t, h1, n1, se1, so1, sz1)
-        maxima(t, se0, so0, sz0, yscale0, col0, True)
-        maxima(t, se1, so1, sz1, yscale1, col1, False)
-        finish(t)
-
-    build(0, ha0, ha1, na0, na1)
-
-    def pair(u, carry):
-        build(2 * u + 1, hb0, hb1, nb0, nb1)
-        one(2 * u, ha0, ha1, na0, na1)
-        build(lax.rem(2 * u + 2, tiles), ha0, ha1, na0, na1)
-        one(2 * u + 1, hb0, hb1, nb0, nb1)
+    def finish(t, racc, i):
+        top = jnp.max(jnp.transpose(racc[L * i : L * i + L, :]), axis=0, keepdims=True)
+        out_ref[pl.ds(4 * t + i, 1), :] = top * xscale[pl.ds(4 * t + i, 1), :]
+
+    def step(product, top, job, rows_of=None, between=None):
+        state = {}
+        for quarter in range(4):
+            half = quarter // 2
+            if quarter % 2 == 0:
+                products(product, half)
+            maxima(top, half, state, range(8 * (quarter % 2), 8 * (quarter % 2) + 8))
+            build(job, quarter)
+            if rows_of is not None:
+                finish(*rows_of, quarter)
+            if quarter == 1 and between is not None:
+                between()
+        close(top, state)
+
+    matrices = ((ha0, na0), (ha1, na1), (hb0, nb0), (hb1, nb1))
+    outputs = ((se0, so0, sz0), (se1, so1, sz1))
+    queries = ((ys1, ytot1, yscale1, col1), (ys0, ytot0, yscale0, col0))
+    raccs = (racc0, racc1, racc2, racc3)
+
+    def tile_of(t, k):
+        return t + k % GROUP if k < 2 * GROUP else lax.rem(t + GROUP + k % GROUP, tiles)
+
+    def matrix_job(t, k):
+        ys, ytot = queries[k // GROUP % 2][:2]
+        return (tile_of(t, k), ys, ytot, *matrices[k % 4])
+
+    def product_job(t, k):
+        return (tile_of(t, k), *matrices[k % 4], outputs[k % 2])
+
+    def maxima_job(t, k):
+        which = k // GROUP % 2
+        return (tile_of(t, k), outputs[k % 2], *queries[which][2:], raccs[k % GROUP], which == 0)
+
+    racc3[...] = jnp.zeros((TILE, L), F32)
+    for quarter in range(4):
+        build(matrix_job(0, 0), quarter)
+    for odd in range(2):
+        products(product_job(0, 0), odd)
+    for k in (1, 2):
+        for quarter in range(4):
+            build(matrix_job(0, k), quarter)
+
+    def group(u, carry):
+        t = GROUP * u
+        pl.when(u > 0)(lambda: give(t - 2, 2, 4))
+
+        @pl.when(u == tiles // GROUP - 1)
+        def _():
+            arrived(0)
+
+            @pl.when(me == count - 1)
+            def _():
+                xf[rows : rows + 8] = jnp.zeros((8, L), F32)
+
+            query(early, tiles)
+
+        for k in range(2 * GROUP):
+            done = None
+            if k == 0:
+                done = (lax.rem(t + tiles - 1, tiles), raccs[GROUP - 1])
+            elif k > GROUP:
+                done = (t + k - GROUP - 1, raccs[k - GROUP - 1])
+            between = None
+            if k == GROUP:
+                between = lambda: give(t, GROUP, 5)
+            elif k == GROUP + 2:
+                between = lambda: give(t, 2, 4)
+            step(product_job(t, k + 1), maxima_job(t, k), matrix_job(t, k + 3), done, between)
         return carry
 
-    lax.fori_loop(0, tiles // 2, pair, 0)
-
+    lax.fori_loop(0, tiles // GROUP, group, 0)
+    give(tiles - 2, 2, 4)
+    for i in range(4):
+        finish(tiles - 1, racc3, i)
     cell = lax.broadcasted_iota(jnp.int32, (rows, L), 0) * L
     cell = cell + lax.broadcasted_iota(jnp.int32, (rows, L), 1)
     keep = me * (rows * L) + cell < valid
@@ -388,7 +456,8 @@
             vm((tiles, 288, TILE), BF16), vm((tiles, 272, TILE), BF16), vm((tiles, TILE, L), F32),
             wide, wide, wide, wide, slots, slots, slots, slots,
             vm((288, TILE), F32), vm((288, TILE), F32), vm((272, TILE), F32), vm((272, TILE), F32),
-            vm((16, L), F32), vm((16, L), F32), vm((TILE, L), F32),
+            vm((16, L), F32), vm((16, L), F32), vm((TILE, L), F32), vm((TILE, L), F32),
+            vm((TILE, L), F32), vm((TILE, L), F32),
             line, line, line, line,
             pltpu.SemaphoreType.DMA((6,)), pltpu.SemaphoreType.DMA((6,)),
             pltpu.SemaphoreType.DMA,
@@ -396,7 +465,7 @@
         compiler_params=pltpu.CompilerParams(
             collective_id=0, has_side_effects=True, vmem_limit_bytes=48 * 2**20
         ),
-    )(series.reshape(rows, L))
+    )(pltpu.with_memory_space_constraint(series.reshape(rows, L), pltpu.HBM))
     return out.reshape(-1)
 
 

time: 31.4 us -> 29.1 us (0.927)
  the two profiles are of different devices: /device:TPU:1 before, /device:TPU:104 now
where the time goes in v4:
time: 29.1 us; the launch traced here: 29 us
  Pallas kernels  28.3 us (97%)
  local copies, waits for them, and re-layouts  0.61 us (2%)
    pallas_call x1, Pallas kernels, per_device(): pl.pallas_call(kernel, out_shape=jax.ShapeDtypeStruct((rows, L), F32), in...  28.3 us
    unnamed x1, local copies, waits for them, and re-layouts  0.61 us

profile of v4, /device:TPU:104, one launch (start us, length us, event | category | flops | bytes accessed | tf_op | source)
XLA Modules:
  0.0 29.0 jit_solution(4617665214331215547)
XLA Ops:
  0.0 28.3 %shard_map.17 = f32[48,128]{1,0:T(8,128)S(1)} custom-call(f32[48,128]{1,0:T(8,128)} %bitcast.3), custom_call_target="tpu_custom_call" | custom-call | tf_op jit(solution)/shard_map/pallas_call | solution.py:447
  28.3 0.6 %copy.3 = f32[6144]{0:T(1024)} copy(f32[6144]{0:T(1024)S(1)} %bitcast.2) | data formatting | bytes 49152

commit v5 on v4

--- a/solution.py
+++ b/solution.py
@@ -169,8 +169,8 @@
     def _():
         pl.semaphore_wait(barrier, listeners)
 
-    for c, p in zip(copies[:4], plan):
-        pl.when(p[3])(c.start)
+    for n in (2, 1, 3, 0):
+        pl.when(plan[n][3])(copies[n].start)
 
     def arrived(n):
         pl.when(plan[n][4])(copies[n].wait_recv)
@@ -358,10 +358,11 @@
         state = {}
         for quarter in range(4):
             half = quarter // 2
-            if quarter % 2 == 0:
+            if quarter % 2 == 0 and product is not None:
                 products(product, half)
             maxima(top, half, state, range(8 * (quarter % 2), 8 * (quarter % 2) + 8))
-            build(job, quarter)
+            if job is not None:
+                build(job, quarter)
             if rows_of is not None:
                 finish(*rows_of, quarter)
             if quarter == 1 and between is not None:
@@ -396,20 +397,7 @@
         for quarter in range(4):
             build(matrix_job(0, k), quarter)
 
-    def group(u, carry):
-        t = GROUP * u
-        pl.when(u > 0)(lambda: give(t - 2, 2, 4))
-
-        @pl.when(u == tiles // GROUP - 1)
-        def _():
-            arrived(0)
-
-            @pl.when(me == count - 1)
-            def _():
-                xf[rows : rows + 8] = jnp.zeros((8, L), F32)
-
-            query(early, tiles)
-
+    def group(t, final):
         for k in range(2 * GROUP):
             done = None
             if k == 0:
@@ -421,10 +409,25 @@
                 between = lambda: give(t, GROUP, 5)
             elif k == GROUP + 2:
                 between = lambda: give(t, 2, 4)
-            step(product_job(t, k + 1), maxima_job(t, k), matrix_job(t, k + 3), done, between)
+            following = None if final and k + 1 >= 2 * GROUP else product_job(t, k + 1)
+            later = None if final and k + 3 >= 2 * GROUP else matrix_job(t, k + 3)
+            step(following, maxima_job(t, k), later, done, between)
+
+    def groups(u, carry):
+        pl.when(u > 0)(lambda: give(GROUP * u - 2, 2, 4))
+        group(GROUP * u, False)
         return carry
 
-    lax.fori_loop(0, tiles // GROUP, group, 0)
+    lax.fori_loop(0, tiles // GROUP - 1, groups, 0)
+    give(tiles - GROUP - 2, 2, 4)
+    arrived(0)
+
+    @pl.when(me == count - 1)
+    def _():
+        xf[rows : rows + 8] = jnp.zeros((8, L), F32)
+
+    query(early, tiles)
+    group(tiles - GROUP, True)
     give(tiles - 2, 2, 4)
     for i in range(4):
         finish(tiles - 1, racc3, i)

time: 29.1 us -> 28.1 us (0.966)
  the two profiles are of different devices: /device:TPU:104 before, /device:TPU:24 now
where the time goes in v5:
time: 28.1 us; the launch traced here: 28 us
  Pallas kernels  27.4 us (98%)
  local copies, waits for them, and re-layouts  0.61 us (2%)
    pallas_call x1, Pallas kernels, per_device(): pl.pallas_call(kernel, out_shape=jax.ShapeDtypeStruct((rows, L), F32), in...  27.4 us
    unnamed x1, local copies, waits for them, and re-layouts  0.61 us

profile of v5, /device:TPU:24, one launch (start us, length us, event | category | flops | bytes accessed | tf_op | source)
XLA Modules:
  0.0 28.0 jit_solution(13495011666957476231)
XLA Ops:
  0.0 27.4 %shard_map.17 = f32[48,128]{1,0:T(8,128)S(1)} custom-call(f32[48,128]{1,0:T(8,128)} %bitcast.3), custom_call_target="tpu_custom_call" | custom-call | tf_op jit(solution)/shard_map/pallas_call | solution.py:450
  27.4 0.6 %copy.3 = f32[6144]{0:T(1024)} copy(f32[6144]{0:T(1024)S(1)} %bitcast.2) | data formatting | bytes 49152

commit v6 on v5

--- a/solution.py
+++ b/solution.py
@@ -413,12 +413,10 @@
             later = None if final and k + 3 >= 2 * GROUP else matrix_job(t, k + 3)
             step(following, maxima_job(t, k), later, done, between)
 
-    def groups(u, carry):
-        pl.when(u > 0)(lambda: give(GROUP * u - 2, 2, 4))
-        group(GROUP * u, False)
-        return carry
-
-    lax.fori_loop(0, tiles // GROUP - 1, groups, 0)
+    for t in range(0, tiles - GROUP, GROUP):
+        if t > 0:
+            give(t - 2, 2, 4)
+        group(t, False)
     give(tiles - GROUP - 2, 2, 4)
     arrived(0)
 

time: 28.1 us -> 28.4 us (1.011)
  Pallas kernels: 27.4 us -> 27.7 us
where the time goes in v6:
time: 28.4 us; the launch traced here: 28.3 us
  Pallas kernels  27.7 us (98%)
  local copies, waits for them, and re-layouts  0.61 us (2%)
    pallas_call x1, Pallas kernels, per_device(): pl.pallas_call(kernel, out_shape=jax.ShapeDtypeStruct((rows, L), F32), in...  27.7 us
    unnamed x1, local copies, waits for them, and re-layouts  0.61 us

profile of v6, /device:TPU:24, one launch (start us, length us, event | category | flops | bytes accessed | tf_op | source)
XLA Modules:
  0.0 28.3 jit_solution(17226940879828104062)
XLA Ops:
  0.0 27.7 %shard_map.17 = f32[48,128]{1,0:T(8,128)S(1)} custom-call(f32[48,128]{1,0:T(8,128)} %bitcast.3), custom_call_target="tpu_custom_call" | custom-call | tf_op jit(solution)/shard_map/pallas_call | solution.py:448
  27.7 0.6 %copy.3 = f32[6144]{0:T(1024)} copy(f32[6144]{0:T(1024)S(1)} %bitcast.2) | data formatting | bytes 49152
